TPU v7x, 512 devices: a whole 4x8x8 slice. The times are simulated.
512 devices in a mesh: grp: 16 (over z, core), dev: 32 (over y, x).
Axes of the slice: x: 4, y: 8, z: 8, core: 2. Of those that a mesh axis runs over, the one named last changes fastest.
Arguments:
- stored_tiles: float32 [512, 33, 128, 128], P(('grp', 'dev')), may hold values from -0.22097087 to 0.22097087, as said below
- tile_flags: int32 [512, 33], P(('grp', 'dev')), may hold values from 0 to 1, as said below
- orbitals: float32 [65536, 256], P(('grp', 'dev')), may hold values from -6 to 6
Outputs:
- product: float32 [65536, 256], P(('grp', 'dev'))
Inputs may be any that keep to these rules, and one draw needn't show every extreme that they name: tile_flags[p, s] is 1 at s = p mod 32, 0 for s below that, and 0 at s = 32 in the last 32 block rows. `stored_tiles`: the tile at slot p mod 32 of block row p is symmetric.
All inputs are finite; a program needn't handle non-finite values.
Results may differ from a plain program's by a relative error of at most 0.000075.
Values sent between devices are 32-bit elements; how exact they have to be, the bound alone decides.
A program may use at most 64 MiB of HBM per device.

v0:
```python
import jax
import jax.numpy as jnp
from jax import lax
from jax.sharding import PartitionSpec as P


def shifted(shard, axis, by):
    count = lax.axis_size(axis)
    pairs = [(i, i + by) for i in range(count) if 0 <= i + by < count]
    return lax.ppermute(shard, axis, pairs)


def per_device(stored_tiles, tile_flags, orbitals):
    highest = lax.Precision.HIGHEST
    group_width = lax.axis_size("dev")
    own_index = lax.axis_index("dev")
    tile_order = stored_tiles.shape[2]
    columns = orbitals.shape[1]
    slot_index = lax.broadcasted_iota(jnp.int32, (group_width,), 0)
    flags_float = tile_flags[0].astype(jnp.float32)
    blocks = stored_tiles[0] * flags_float[:, None, None]
    in_group = blocks[:group_width]
    next_tile = blocks[group_width]
    beside = in_group * (slot_index != own_index).astype(jnp.float32)[:, None, None]
    piece_rows = lax.all_gather(orbitals, "dev", axis=0, tiled=True)
    num_slots = piece_rows.shape[0] // tile_order
    x_rows = piece_rows.reshape(num_slots, tile_order, columns)
    product = jnp.einsum("sij,sjk->ik", in_group, x_rows, precision=highest)
    row_count = lax.axis_size("dev") * orbitals.shape[0]
    terms = jnp.einsum("sji,jk->sik", beside, orbitals, precision=highest)
    product = product + lax.psum_scatter(
        terms.reshape(row_count, columns), "dev", scatter_dimension=0, tiled=True
    )
    following = shifted(orbitals, "grp", -1)
    product = product + jnp.dot(next_tile, following, precision=highest)
    upward = jnp.einsum("ji,jk->ik", next_tile, orbitals, precision=highest)
    product = product + shifted(upward, "grp", 1)
    return product


def solution(mesh):
    in_specs = (
        P(("grp", "dev"), None, None, None),
        P(("grp", "dev"), None),
        P(("grp", "dev"), None),
    )
    out_specs = P(("grp", "dev"), None)
    return jax.shard_map(
        per_device, mesh=mesh, in_specs=in_specs, out_specs=out_specs, check_vma=False
    )
```

profile of v0, /device:TPU:16, one launch (start us, length us, event | category | flops | bytes accessed | tf_op | source)
XLA Modules:
  0.0 342.0 jit_solution(7017481486420995727)
XLA Ops:
  6.5 0.0 all-gather.2.cloned.1.call-start
  6.5 0.7 all-gather.2.cloned.1.call-update
  7.3 0.0 reduce-scatter.2.cloned.1.call-start
  7.3 0.7 convert_bitcast_fusion
  8.0 0.0 copy-start
  8.0 1.8 bitcast_multiply_fusion
  9.8 0.0 copy-done
  9.8 5.7 %fusion = f32[32,128,256]{2,1,0:T(8,128)} fusion(f32[33,128,128]{2,1,0:T(8,128)S(1)} %bitcast_multiply_fusion, f32[32]{0:T(128)S(1)} %compare_convert_fusion, f32[128,256]{1,0:T(8,128)S(1)} %copy-done), kind=kOutput, calls=%fused_computation.2 | convolution fusion | flops 1611137024 | bytes 6423040 | tf_op jit(solution)/shard_map/sji,jk->sik/dot_general | solution.py:30
  15.5 0.0 reduce-scatter.2.cloned.1.call-update
  15.6 1.3 collective-permute-start
  16.9 0.3 fusion.5
  17.2 3.0 collective-permute-start.1
  20.2 80.8 %all-gather.2.cloned.1.call-done = f32[4096,256]{1,0:T(8,128)} async-done(((f32[128,256]{1,0:T(8,128)}), f32[4096,256]{1,0:T(8,128)}) %all-gather.2.cloned.1.call-update) | async-done | bytes 4194320 | tf_op jit(solution)/shard_map/all_gather | solution.py:25
  101.0 229.2 %reduce-scatter.2.cloned.1.call-done = f32[128,256]{1,0:T(8,128)} async-done(((f32[4096,256]{1,0:T(8,128)}), f32[128,256]{1,0:T(8,128)}) %reduce-scatter.2.cloned.1.call-update) | async-done | bytes 131088 | tf_op jit(solution)/shard_map/reduce_scatter | solution.py:31
  330.2 3.9 %fusion.2 = f32[128,256]{1,0:T(8,128)S(1)} fusion(f32[128,256]{1,0:T(8,128)} %reduce-scatter.2.cloned.1.call-done, f32[33,128,128]{2,1,0:T(8,128)S(1)} %bitcast_multiply_fusion, f32[32,128,256]{2,1,0:T(8,128)} %bitcast.22), kind=kOutput, calls=%fused_computation.6 | convolution fusion | flops 1610645504 | bytes 6619136 | tf_op jit(solution)/shard_map/sij,sjk->ik/dot_general | solution.py:28
  334.2 0.0 collective-permute-done.1
  334.2 0.0 collective-permute-done
  334.2 0.9 fusion.1
  (1 shorter events, 0.0 us)
Async XLA Ops:
  6.5 94.5 %all-gather.2.cloned.1.call-start = ((), (), s32[]{:S(2)}) async-start(), calls=%async_computation.1 | async-start | bytes 4325376 | tf_op jit(solution)/shard_map/all_gather | solution.py:25
  7.3 323.0 %reduce-scatter.2.cloned.1.call-start = ((), (), s32[]{:S(2)}) async-start(), calls=%async_computation.2 | async-start | bytes 4325376 | tf_op jit(solution)/shard_map/reduce_scatter | solution.py:31
  8.0 1.9 copy-start
  15.6 318.6 %collective-permute-start = (f32[128,256]{1,0:T(8,128)S(1)}, f32[128,256]{1,0:T(8,128)S(1)}, u32[]{:S(2)}, u32[]{:S(2)}) collective-permute-start(f32[128,256]{1,0:T(8,128)S(1)} %copy-done), channel_id=1, source_target_pairs={{32,0},{64,32},{96,64},{128,96},{160,128},{192,160},{224,192},{256... | collective-permute-start | bytes 393224 | tf_op jit(solution)/shard_map/ppermute | solution.py:10
  17.2 317.0 %collective-permute-start.1 = (f32[128,256]{1,0:T(8,128)S(1)}, f32[128,256]{1,0:T(8,128)S(1)}, u32[]{:S(2)}, u32[]{:S(2)}) collective-permute-start(f32[128,256]{1,0:T(8,128)S(1)} %fusion.5), channel_id=1, source_target_pairs={{0,32},{32,64},{64,96},{96,128},{128,160},{160,192},{192,224},{224... | collective-permute-start | bytes 393224 | tf_op jit(solution)/shard_map/ppermute | solution.py:10
Sparse Core Ops, SparseCore 0:
  10.5 90.4 all-gather.1
  105.5 224.7 reduce-scatter.1
where the time goes:
time: 342 us
  waiting for transfers between devices  311 us (91%)
  between operations  13.5 us (4%)
  matrix products  10.9 us (3%)
  starting transfers between devices  4.37 us (1%)
    reduce_scatter x1, waiting for transfers between devices, per_device(): lax.psum_scatter(terms.reshape(row_count, columns), 'dev', scatter_dimens...  229 us
    all_gather x1, waiting for transfers between devices, per_device(): piece_rows = lax.all_gather(orbitals, 'dev', axis=0, tiled=True)  80.8 us
  transfers between devices with their start and end apart: 4, of which 2 were waited for; matrix products, arithmetic and copies ran while one was open for 4% of the time, Pallas kernels for 0%

commit v1 on v0

v1 whole, which is shorter than its diff:
```python
import jax
import jax.numpy as jnp
from jax import lax
from jax.experimental import pallas as pl
from jax.experimental.pallas import tpu as pltpu
from jax.sharding import PartitionSpec as P

MESH = pl.DeviceIdType.MESH
NX = 4
NY = 8


def split(v):
    high = v.astype(jnp.bfloat16)
    return high, (v - high.astype(jnp.float32)).astype(jnp.bfloat16)


def multiply(a, b, dims):
    def one(u, v):
        return lax.dot_general(u, v, (dims, ((), ())), preferred_element_type=jnp.float32)

    return one(a[0], b[0]) + (one(a[0], b[1]) + one(a[1], b[0]))


PLAIN = ((1,), (0,))
TURNED = ((0,), (0,))


def kernel(
    tiles, flags, orb, out,
    own, held, xrow, xrow_high, xrow_low, xcol, total, mirror_out, mirror_in, direct_in, x_next, up_out, up_in,
    load_sem, tile_send, tile_recv, xrow_send, xrow_recv, xcol_send, xcol_recv,
    mirror_send, mirror_recv, direct_send, direct_recv, next_send, next_recv,
):
    order = tiles.shape[1]
    slots = tiles.shape[0]
    groups = lax.axis_size("grp")
    g, d = lax.axis_index("grp"), lax.axis_index("dev")
    y, x = d // NX, d % NX

    def in_row(j):
        return {"dev": y * NX + (x + j) % NX}

    def in_column(k):
        return {"dev": (y + k) * NX + x}

    def block(i):
        return pl.ds(pl.multiple_of(i * order, order), order)

    def remote(src, dst, send, recv, device):
        return pltpu.make_async_remote_copy(
            src_ref=src, dst_ref=dst, send_sem=send, recv_sem=recv, device_id=device, device_id_type=MESH
        )

    def tile_copy(j, k):
        return remote(
            own.at[(y + k) * NX + (x + j) % NX], held.at[k, block(x)],
            tile_send.at[j, k], tile_recv.at[j, k], in_row(j),
        )

    def xrow_copy(j):
        return remote(orb, xrow.at[block(x)], xrow_send.at[j], xrow_recv.at[j], in_row(j))

    def xcol_copy(k):
        return remote(orb, xcol.at[k], xcol_send.at[k], xcol_recv.at[k], in_column(-k))

    def mirror_copy(k):
        return remote(mirror_out.at[k], mirror_in.at[k], mirror_send.at[k], mirror_recv.at[k], in_column(k))

    def direct_copy(j):
        return remote(
            total.at[block((x + j) % NX)], direct_in.at[j], direct_send.at[j], direct_recv.at[j], in_row(j)
        )

    def back_copy():
        return remote(orb, x_next, next_send.at[0], next_recv.at[0], {"grp": g - 1})

    def up_copy():
        return remote(up_out, up_in, next_send.at[1], next_recv.at[1], {"grp": g + 1})

    def step_of(i):
        return (4 + jnp.where(i % 2 == 1, (i + 1) // 2, -(i // 2)) + NY) % NY

    load_tiles = pltpu.make_async_copy(tiles, own, load_sem.at[0])
    load_row = pltpu.make_async_copy(orb, xrow.at[block(x)], load_sem.at[1])
    load_col = pltpu.make_async_copy(orb, xcol.at[0], load_sem.at[2])
    load_tiles.start()
    load_row.start()
    load_col.start()
    held[0] = jnp.zeros_like(held[0])

    barrier = pltpu.get_barrier_semaphore()
    for j in range(1, NX):
        pl.semaphore_signal(barrier, inc=1, device_id=in_row(j), device_id_type=MESH)
    for k in range(1, NY):
        pl.semaphore_signal(
            barrier, inc=1, device_id={"dev": ((y + k) % NY) * NX + x}, device_id_type=MESH
        )

    for i in (1, groups - 1):
        pl.semaphore_signal(
            barrier, inc=1, device_id={"grp": (g + i) % groups}, device_id_type=MESH
        )

    load_tiles.wait()

    def mask(s, carry):
        own[s] = own[s] * flags[0, s].astype(jnp.float32)
        return carry

    lax.fori_loop(y * NX, slots, mask, 0)

    pl.semaphore_wait(barrier, NX - 1 + NY - 1 + 2)

    for j in range(1, NX):
        xrow_copy(j).start()

    def send_xcol(i, carry):
        k = step_of(i)

        @pl.when(k <= y)
        def _():
            xcol_copy(k).start()

        return carry

    lax.fori_loop(0, NY - 1, send_xcol, 0)

    @pl.when(g > 0)
    def _():
        back_copy().start()

    def send_tiles(i, carry):
        k = step_of(i)

        @pl.when(y + k < NY)
        def _():
            for j in range(1, NX):
                tile_copy(j, k).start()

        return carry

    lax.fori_loop(0, NY - 1, send_tiles, 0)
    for j in range(1, NX):

        @pl.when(x + j < NX)
        def _():
            tile_copy(j, 0).start()

    load_row.wait()
    load_col.wait()
    x_own = split(xcol[0])

    @pl.when(g < groups - 1)
    def _():
        up_out[...] = multiply(split(own[slots - 1]), x_own, TURNED)
        up_copy().start()

    def place(k, carry):
        held[k, block(x)] = own[(y + k) * NX + x]
        return carry

    lax.fori_loop(0, NY - y, place, 0)
    total[...] = jnp.zeros_like(total)
    for j in range(1, NX):
        xrow_copy(j).wait_recv()
    xrow_high[...], xrow_low[...] = split(xrow[...])

    def step(i, carry):
        k = step_of(i)

        @pl.when(y + k < NY)
        def _():
            xcol_copy(k).wait_recv()
            for j in range(1, NX):
                tile_copy(j, k).wait_recv()
            here = split(held[k])
            mirror_out[k] = multiply(here, (xrow_high[...], xrow_low[...]), TURNED)
            mirror_copy(k).start()
            total[...] += multiply(here, split(xcol[k]), PLAIN)

        return carry

    lax.fori_loop(0, NY - 1, step, 0)

    for j in range(1, NX):

        @pl.when(x - j >= 0)
        def _():
            tile_copy(j, 0).wait_recv()

    total[...] += multiply(split(held[0]), x_own, PLAIN)
    for j in range(1, NX):
        direct_copy(j).start()
    held[0, block(x)] = jnp.zeros((order, order), jnp.float32)
    out[...] = total[block(x)] + multiply(split(held[0]), (xrow_high[...], xrow_low[...]), TURNED)

    @pl.when(g < groups - 1)
    def _():
        back_copy().wait_recv()
        out[...] += multiply(split(own[slots - 1]), split(x_next[...]), PLAIN)

    @pl.when(g > 0)
    def _():
        up_copy().wait_recv()
        out[...] += up_in[...]

    def take(i, carry):
        k = step_of(i)

        @pl.when(k <= y)
        def _():
            mirror_copy(k).wait_recv()
            out[...] += mirror_in[k]

        return carry

    lax.fori_loop(0, NY - 1, take, 0)
    for j in range(1, NX):
        direct_copy(j).wait_recv()
        out[...] += direct_in[j]

    for j in range(1, NX):
        xrow_copy(j).wait_send()
        direct_copy(j).wait_send()

        @pl.when(x + j < NX)
        def _():
            tile_copy(j, 0).wait_send()

    def finish(k, carry):
        @pl.when(k <= y)
        def _():
            xcol_copy(k).wait_send()

        @pl.when(y + k < NY)
        def _():
            mirror_copy(k).wait_send()
            for j in range(1, NX):
                tile_copy(j, k).wait_send()

        return carry

    lax.fori_loop(1, NY, finish, 0)

    @pl.when(g > 0)
    def _():
        back_copy().wait_send()

    @pl.when(g < groups - 1)
    def _():
        up_copy().wait_send()


def per_device(stored_tiles, tile_flags, orbitals):
    slots, order = stored_tiles.shape[1:3]
    columns = orbitals.shape[1]
    f32, bf16 = jnp.float32, jnp.bfloat16
    dma = pltpu.SemaphoreType.DMA
    return pl.pallas_call(
        kernel,
        out_shape=jax.ShapeDtypeStruct(orbitals.shape, f32),
        in_specs=[
            pl.BlockSpec(memory_space=pl.ANY),
            pl.BlockSpec(memory_space=pltpu.SMEM),
            pl.BlockSpec(memory_space=pl.ANY),
        ],
        out_specs=pl.BlockSpec(memory_space=pltpu.VMEM),
        scratch_shapes=[
            pltpu.VMEM((slots, order, order), f32),
            pltpu.VMEM((NY, NX * order, order), f32),
            pltpu.VMEM((NX * order, columns), f32),
            pltpu.VMEM((NX * order, columns), bf16),
            pltpu.VMEM((NX * order, columns), bf16),
            pltpu.VMEM((NY, order, columns), f32),
            pltpu.VMEM((NX * order, columns), f32),
            pltpu.VMEM((NY, order, columns), f32),
            pltpu.VMEM((NY, order, columns), f32),
            pltpu.VMEM((NX, order, columns), f32),
            pltpu.VMEM((order, columns), f32),
            pltpu.VMEM((order, columns), f32),
            pltpu.VMEM((order, columns), f32),
            dma((3,)),
            dma((NX, NY)),
            dma((NX, NY)),
            dma((NX,)),
            dma((NX,)),
            dma((NY,)),
            dma((NY,)),
            dma((NY,)),
            dma((NY,)),
            dma((NX,)),
            dma((NX,)),
            dma((2,)),
            dma((2,)),
        ],
        compiler_params=pltpu.CompilerParams(
            collective_id=0, has_side_effects=True, vmem_limit_bytes=63 << 20
        ),
    )(stored_tiles[0], tile_flags, orbitals)


def solution(mesh):
    in_specs = (
        P(("grp", "dev"), None, None, None),
        P(("grp", "dev"), None),
        P(("grp", "dev"), None),
    )
    out_specs = P(("grp", "dev"), None)
    return jax.shard_map(
        per_device, mesh=mesh, in_specs=in_specs, out_specs=out_specs, check_vma=False
    )
```

time: 342 us -> 49.5 us (0.14)
  the two profiles are of different devices: /device:TPU:16 before, /device:TPU:4 now
where the time goes in v1:
time: 49.5 us; the launch traced here: 49.3 us
  Pallas kernels  47.8 us (97%)
  local copies, waits for them, and re-layouts  1.57 us (3%)
    pallas_call x1, Pallas kernels, per_device(): pl.pallas_call(kernel, out_shape=jax.ShapeDtypeStruct(orbitals.shape, f32...  47.8 us
    unnamed x1, local copies, waits for them, and re-layouts  1.57 us

profile of v1, /device:TPU:4, one launch (start us, length us, event | category | flops | bytes accessed | tf_op | source)
XLA Modules:
  0.0 49.3 jit_solution(3043595205928485785)
XLA Ops:
  0.0 47.8 %shard_map.37 = f32[128,256]{1,0:T(8,128)} custom-call(f32[33,128,128]{2,1,0:T(8,128)} %bitcast.1, s32[1,33]{1,0:T(1,128)} %flags.1, f32[128,256]{1,0:T(8,128)} %orb.1), custom_call_target="tpu_custom_call" | custom-call | tf_op jit(solution)/shard_map/pallas_call | solution.py:260
  47.8 1.6 %copy.5 = f32[128,256]{1,0:T(8,128)} copy(f32[128,256]{1,0:T(8,128)} %shard_map.37) | data formatting | bytes 262144

commit v2 on v1

v2 whole, which is shorter than its diff:
```python
import jax
import jax.numpy as jnp
from jax import lax
from jax.experimental import pallas as pl
from jax.experimental.pallas import tpu as pltpu
from jax.sharding import PartitionSpec as P

MESH = pl.DeviceIdType.MESH
NX = 4
NY = 8
HALF = NY // 2
MIDDLE = HALF - 1
TILE_ORDER = (4, 5, 3, 6, 2, 1)
WINDOW = 3


TURNED_STEPS = (1, NY - 1)
TURNED_ROWS = 2


def turned(y, k):
    return (y >= 0) & (y + k < NY) & ((k == NY - 1) | ((k == 1) & (y < TURNED_ROWS)))


def straight(y, k):
    return (y >= 0) & (y + k < NY) & (k >= 1) & (turned(y, k) ^ True)


def passed(y, k):
    return straight(y, k) & (((k < HALF) & (y >= 1) & (y != HALF)) | (k > HALF + 1))


def forwards(y, k):
    return (y + k < NY) & (k <= HALF) & (y >= (2 if k == HALF else 1))


def sent_units(y):
    steps = sum(bool(straight(y, k)) for k in range(1, NY))
    given = sum(bool(turned(y, k)) for k in TURNED_STEPS)
    taken = sum(bool(turned(y - k, k)) for k in TURNED_STEPS)
    down = sum(bool(forwards(y, k)) for k in range(1, HALF + 1))
    along_row = (NX - 1) * (2 + 2 + steps)
    along_column = 2 * ((y >= 2) + (y > HALF) + down + steps + taken) + (NX + 2) * given
    return along_row, along_column


def split(v):
    high = v.astype(jnp.bfloat16)
    return high, (v - high.astype(jnp.float32)).astype(jnp.bfloat16)


def multiply(a, b, dims):
    def one(u, v):
        return lax.dot_general(u, v, (dims, ((), ())), preferred_element_type=jnp.float32)

    return one(a[0], b[0]) + (one(a[0], b[1]) + one(a[1], b[0]))


PLAIN = ((1,), (0,))
TURNED = ((0,), (0,))


def kernel(
    tiles, flags, orb, out,
    own, held, xrow, xrow_high, xrow_low, xcol, total, mirror_out, mirror_in, direct_in, x_next, up_out, up_in,
    flags_here, turned_tiles, turned_x, back_out, back_in,
    load_sem, row_send, column_send, next_send,
    tile_recv, xrow_recv, xcol_recv, mirror_recv, direct_recv, next_recv, turned_recv, token,
):
    order = tiles.shape[1]
    slots = tiles.shape[0]
    groups = lax.axis_size("grp")
    g, d = lax.axis_index("grp"), lax.axis_index("dev")
    y, x = d // NX, d % NX

    def in_row(j):
        return {"dev": y * NX + (x + j) % NX}

    def in_column(k):
        return {"dev": (y + k) * NX + x}

    def block(i):
        return pl.ds(pl.multiple_of(i * order, order), order)

    def remote(src, dst, send, recv, device):
        return pltpu.make_async_remote_copy(
            src_ref=src, dst_ref=dst, send_sem=send, recv_sem=recv, device_id=device, device_id_type=MESH
        )

    def tile_copy(j, k):
        return remote(
            own.at[(y + k) * NX + (x + j) % NX], held.at[k, block(x)],
            row_send.at[0], tile_recv.at[k - 1], in_row(j),
        )

    def done(units, send, recv):
        return remote(own.at[pl.ds(0, units)], own.at[pl.ds(0, units)], send, recv, in_row(1))

    def xrow_copy(j):
        return remote(orb, xrow.at[block(x)], row_send.at[0], xrow_recv.at[0], in_row(j))

    def at(row):
        return {"dev": row * NX + x}

    def half(ref, h):
        return ref.at[pl.ds(h * (order // 2), order // 2)]

    def xcol_send_half(src, k, h, row):
        return remote(half(src, h), half(xcol.at[k], h), column_send.at[0], xcol_recv.at[k - 1, h], at(row))

    def xcol_first(h):
        return xcol_send_half(orb, 1, h, y - 1)

    def xcol_round(h):
        first = y < NY - 1
        return xcol_send_half(orb, jnp.where(first, y, y - 1), h, jnp.where(first, 0, 1))

    def xcol_down(k, h):
        return xcol_send_half(xcol.at[k], k + 1, h, y - 1)

    def xcol_arrival(k, h):
        return xcol_send_half(orb, k, h, y)

    def forward_down(k):
        for h in range(2):

            @pl.when(forwards(y, k))
            def _():
                xcol_arrival(k, h).wait_recv()
                xcol_down(k, h).start()

    def mirror_copy(k):
        if k <= HALF:
            on, beyond = passed(y + 1, k - 1), y + 1
            place = jnp.where(on, k - 1, jnp.where((y == MIDDLE) & (k > 1), HALF + 1, 0))
        else:
            on, beyond, place = passed(y - 1, k + 1), y - 1, HALF
        row = jnp.where(on, beyond, y + k)
        return remote(mirror_out.at[k], mirror_in.at[place], column_send.at[0], mirror_recv.at[place], at(row))

    def mirror_arrival(i):
        return remote(orb, mirror_in.at[i], column_send.at[0], mirror_recv.at[i], at(y))

    def direct_copy(j):
        return remote(
            total.at[block((x + j) % NX)], direct_in.at[j], row_send.at[0], direct_recv.at[0], in_row(j)
        )

    def back_copy():
        return remote(orb, x_next, next_send.at[0], next_recv.at[0], {"grp": g - 1})

    def up_copy():
        return remote(up_out, up_in, next_send.at[1], next_recv.at[1], {"grp": g + 1})

    def turned_tile_copy(e, k):
        return remote(
            own.at[pl.ds((y + k) * NX, NX)], turned_tiles.at[e], column_send.at[0], turned_recv.at[0], in_column(k)
        )

    def turned_x_copy(e, k):
        return remote(orb, turned_x.at[e], column_send.at[0], turned_recv.at[0], in_column(k))

    def turned_back_copy(e, k):
        return remote(back_out.at[e], back_in.at[e], column_send.at[0], turned_recv.at[1 + e], in_column(-k))

    load_tiles = pltpu.make_async_copy(tiles, own, load_sem.at[0])
    load_row = pltpu.make_async_copy(orb, xrow.at[block(x)], load_sem.at[1])
    load_col = pltpu.make_async_copy(orb, xcol.at[0], load_sem.at[2])
    load_flags = pltpu.make_async_copy(flags, flags_here, load_sem.at[3])
    load_flags.start()
    load_tiles.start()
    load_row.start()
    load_col.start()

    def greet(condition, semaphore, row):
        @pl.when(condition)
        def _():
            pl.semaphore_signal(semaphore, inc=1, device_id=at(row), device_id_type=MESH)

    barrier = pltpu.get_barrier_semaphore()
    for j in range(1, NX):
        pl.semaphore_signal(barrier, inc=1, device_id=in_row(j), device_id_type=MESH)
    greet(y > 0, barrier, y - 1)
    greet(y < NY - 1, barrier, y + 1)
    greet(y > HALF, barrier, MIDDLE)
    for row in range(HALF + 1, NY):
        greet(y == MIDDLE, barrier, row)

    @pl.when(g > 0)
    def _():
        pl.semaphore_signal(barrier, inc=1, device_id={"grp": g - 1}, device_id_type=MESH)

    @pl.when(g < groups - 1)
    def _():
        pl.semaphore_signal(barrier, inc=1, device_id={"grp": g + 1}, device_id_type=MESH)

    load_flags.wait()
    load_tiles.wait()

    def mask(s, carry):
        own[s] = own[s] * flags_here[0, s].astype(jnp.float32)
        return carry

    lax.fori_loop(y * NX, slots, mask, 0)

    peers = NX - 1
    for condition in (g > 0, g < groups - 1, y > 0, y < NY - 1, y > HALF):
        peers = peers + condition.astype(jnp.int32)
    peers = peers + jnp.where(y == MIDDLE, NY - 1 - HALF, 0)
    pl.semaphore_wait(barrier, peers)

    @pl.when(y >= 2)
    def _():
        xcol_first(0).start()
        xcol_first(1).start()

    for j in (2, 1, 3):
        xrow_copy(j).start()

    @pl.when(turned(y, 1))
    def _():
        turned_tile_copy(0, 1).start()
        turned_x_copy(0, 1).start()

    @pl.when(g > 0)
    def _():
        back_copy().start()

    def send_tiles(k):
        @pl.when(straight(y, k))
        def _():
            for j in (2, 1, 3):
                tile_copy(j, k).start()

    for k in TILE_ORDER[:WINDOW]:
        send_tiles(k)

    greet(y == 0, token.at[0], 1)
    greet(y == MIDDLE, token.at[1], MIDDLE - 1)

    @pl.when((y > 0) & (y <= MIDDLE))
    def _():
        pl.semaphore_wait(token.at[0], 1)

    greet((y > 0) & (y < MIDDLE), token.at[0], y + 1)
    for row in range(HALF + 1, NY):
        greet(y == MIDDLE, token.at[0], row)

    load_row.wait()
    load_col.wait()
    x_own = split(xcol[0])

    @pl.when(g < groups - 1)
    def _():
        up_out[...] = multiply(split(own[slots - 1]), x_own, TURNED)
        up_copy().start()

    def place(k, carry):
        held[k, block(x)] = own[(y + k) * NX + x]
        return carry

    lax.fori_loop(1, NY - y, place, 0)
    beside = jnp.concatenate([own[y * NX + b] for b in range(NX)], axis=1)
    column = lax.broadcasted_iota(jnp.int32, beside.shape, 1)
    total[...] = multiply(
        split(jnp.where(column // order == x, 0.0, beside)), x_own, TURNED
    )
    forward_down(1)

    @pl.when(y < MIDDLE)
    def _():
        pl.semaphore_wait(token.at[1], 1)

    greet((y > 0) & (y < MIDDLE), token.at[1], y - 1)

    @pl.when(turned(y, NY - 1))
    def _():
        turned_tile_copy(1, NY - 1).start()
        turned_x_copy(1, NY - 1).start()

    forward_down(2)

    @pl.when(y > HALF)
    def _():
        pl.semaphore_wait(token.at[0], 1)
        xcol_round(0).start()
        xcol_round(1).start()

    forward_down(3)
    done(2 * (NX - 1), row_send.at[0], xrow_recv.at[0]).wait_recv()
    xrow_high[...], xrow_low[...] = split(xrow[...])
    out[...] = multiply(split(beside), (xrow_high[...], xrow_low[...]), PLAIN)

    def await_tiles(k):
        @pl.when(straight(y, k))
        def _():
            done(NX - 1, row_send.at[0], tile_recv.at[k - 1]).wait_recv()

        later = TILE_ORDER.index(k) + WINDOW
        if later < len(TILE_ORDER):
            send_tiles(TILE_ORDER[later])

    def mirror_step(k):
        @pl.when(straight(y, k))
        def _():
            mirror_out[k] = multiply(split(held[k]), (xrow_high[...], xrow_low[...]), TURNED)

    def pass_step(k):
        @pl.when(passed(y, k))
        def _():
            mirror_arrival(min(k, HALF)).wait_recv()
            mirror_out[k] += mirror_in[min(k, HALF)]

        @pl.when(straight(y, k))
        def _():
            mirror_copy(k).start()

    def direct_step(k):
        @pl.when(straight(y, k) & (forwards(y, k) ^ True))
        def _():
            xcol_arrival(k, 0).wait_recv()
            xcol_arrival(k, 1).wait_recv()

        @pl.when(straight(y, k))
        def _():
            total[...] += multiply(split(held[k]), split(xcol[k]), PLAIN)

    def send_direct():
        for j in (2, 1, 3):
            direct_copy(j).start()

    for k in (4, 5):
        await_tiles(k)
        mirror_step(k)
        pass_step(k)
        if k == HALF:
            forward_down(4)
    for e, k in enumerate(TURNED_STEPS):

        @pl.when(turned(y - k, k))
        def _():
            done(NX + 2, column_send.at[0], turned_recv.at[0]).wait_recv()
            wide = split(jnp.concatenate([turned_tiles[e, b] for b in range(NX)], axis=1))
            back_out[e] = multiply(wide, (xrow_high[...], xrow_low[...]), PLAIN)
            turned_back_copy(e, k).start()
            total[...] += multiply(wide, split(turned_x[e]), TURNED)

    @pl.when(g < groups - 1)
    def _():
        back_copy().wait_recv()
        out[...] += multiply(split(own[slots - 1]), split(x_next[...]), PLAIN)

    @pl.when(g > 0)
    def _():
        up_copy().wait_recv()
        out[...] += up_in[...]

    await_tiles(3)
    mirror_step(3)
    pass_step(3)
    direct_step(4)
    await_tiles(6)
    mirror_step(6)
    direct_step(5)
    direct_step(3)
    direct_step(6)
    await_tiles(2)
    mirror_step(2)
    pass_step(2)
    direct_step(2)

    @pl.when(y < TURNED_ROWS)
    def _():
        send_direct()

    pass_step(6)
    await_tiles(1)
    direct_step(1)

    @pl.when(y >= TURNED_ROWS)
    def _():
        send_direct()

    mirror_step(1)
    pass_step(1)
    out[...] += total[block(x)]

    for e, k in enumerate(TURNED_STEPS):

        @pl.when(turned(y, k))
        def _():
            turned_back_copy(e, k).wait_recv()
            out[...] += back_in[e]

    @pl.when(y > HALF)
    def _():
        mirror_arrival(HALF).wait_recv()
        mirror_arrival(HALF + 1).wait_recv()
        out[...] += mirror_in[HALF] + mirror_in[HALF + 1]

    @pl.when(y >= 2)
    def _():
        mirror_arrival(0).wait_recv()
        out[...] += mirror_in[0]

    done(2 * (NX - 1), row_send.at[0], direct_recv.at[0]).wait_recv()
    out[...] += direct_in[1] + direct_in[2] + direct_in[3]

    for row in range(NY):

        @pl.when(y == row)
        def _():
            along_row, along_column = sent_units(row)
            done(along_row, row_send.at[0], xrow_recv.at[0]).wait_send()
            done(along_column, column_send.at[0], xrow_recv.at[0]).wait_send()

    @pl.when(g > 0)
    def _():
        back_copy().wait_send()

    @pl.when(g < groups - 1)
    def _():
        up_copy().wait_send()


def per_device(stored_tiles, tile_flags, orbitals):
    slots, order = stored_tiles.shape[1:3]
    columns = orbitals.shape[1]
    f32, bf16 = jnp.float32, jnp.bfloat16
    dma = pltpu.SemaphoreType.DMA
    return pl.pallas_call(
        kernel,
        out_shape=jax.ShapeDtypeStruct(orbitals.shape, f32),
        in_specs=[pl.BlockSpec(memory_space=pl.ANY)] * 3,
        out_specs=pl.BlockSpec(memory_space=pltpu.VMEM),
        scratch_shapes=[
            pltpu.VMEM((slots, order, order), f32),
            pltpu.VMEM((NY, NX * order, order), f32),
            pltpu.VMEM((NX * order, columns), f32),
            pltpu.VMEM((NX * order, columns), bf16),
            pltpu.VMEM((NX * order, columns), bf16),
            pltpu.VMEM((NY, order, columns), f32),
            pltpu.VMEM((NX * order, columns), f32),
            pltpu.VMEM((NY, order, columns), f32),
            pltpu.VMEM((HALF + 2, order, columns), f32),
            pltpu.VMEM((NX, order, columns), f32),
            pltpu.VMEM((order, columns), f32),
            pltpu.VMEM((order, columns), f32),
            pltpu.VMEM((order, columns), f32),
            pltpu.SMEM(tile_flags.shape, jnp.int32),
            pltpu.VMEM((2, NX, order, order), f32),
            pltpu.VMEM((2, order, columns), f32),
            pltpu.VMEM((2, order, columns), f32),
            pltpu.VMEM((2, order, columns), f32),
            dma((4,)),
            dma((1,)),
            dma((1,)),
            dma((2,)),
            dma((NY - 2,)),
            dma((1,)),
            dma((NY - 2, 2)),
            dma((HALF + 2,)),
            dma((1,)),
            dma((2,)),
            dma((3,)),
            pltpu.SemaphoreType.REGULAR((2,)),
        ],
        compiler_params=pltpu.CompilerParams(
            collective_id=0, has_side_effects=True, vmem_limit_bytes=48 << 20
        ),
    )(*(pltpu.with_memory_space_constraint(v, pltpu.HBM) for v in (stored_tiles[0], tile_flags, orbitals)))


def solution(mesh):
    in_specs = (
        P(("grp", "dev"), None, None, None),
        P(("grp", "dev"), None),
        P(("grp", "dev"), None),
    )
    out_specs = P(("grp", "dev"), None)
    return jax.shard_map(
        per_device, mesh=mesh, in_specs=in_specs, out_specs=out_specs, check_vma=False
    )
```

time: 49.5 us -> 38.9 us (0.79)
  the two profiles are of different devices: /device:TPU:4 before, /device:TPU:26 now
where the time goes in v2:
time: 38.9 us; the launch traced here: 38.7 us
  Pallas kernels  38.1 us (98%)
  local copies, waits for them, and re-layouts  0.66 us (2%)
    pallas_call x1, Pallas kernels, per_device(): pl.pallas_call(kernel, out_shape=jax.ShapeDtypeStruct(orbitals.shape, f32...  38.1 us

profile of v2, /device:TPU:26, one launch (start us, length us, event | category | flops | bytes accessed | tf_op | source)
XLA Modules:
  0.0 38.7 jit_solution(1957739747671673448)
XLA Ops:
  0.0 38.1 %shard_map.37 = f32[128,256]{1,0:T(8,128)S(1)} custom-call(f32[33,128,128]{2,1,0:T(8,128)} %bitcast.1, s32[1,33]{1,0:T(1,128)} %flags.1, f32[128,256]{1,0:T(8,128)} %orb.1), custom_call_target="tpu_custom_call" | custom-call | tf_op jit(solution)/shard_map/pallas_call | solution.py:431
  38.1 0.7 %copy.5 = f32[128,256]{1,0:T(8,128)} copy(f32[128,256]{1,0:T(8,128)S(1)} %shard_map.37) | data formatting | bytes 262144

commit v3 on v2

--- a/solution.py
+++ b/solution.py
@@ -11,7 +11,7 @@
 HALF = NY // 2
 MIDDLE = HALF - 1
 TILE_ORDER = (4, 5, 3, 6, 2, 1)
-WINDOW = 3
+WINDOW = 4
 
 
 TURNED_STEPS = (1, NY - 1)

time: 38.9 us -> 38.9 us (level)
  the two profiles are of different devices: /device:TPU:26 before, /device:TPU:152 now
where the time goes in v3:
time: 38.9 us; the launch traced here: 38.8 us
  Pallas kernels  38.1 us (98%)
  local copies, waits for them, and re-layouts  0.66 us (2%)
    pallas_call x1, Pallas kernels, per_device(): pl.pallas_call(kernel, out_shape=jax.ShapeDtypeStruct(orbitals.shape, f32...  38.1 us

profile of v3, /device:TPU:152, one launch (start us, length us, event | category | flops | bytes accessed | tf_op | source)
XLA Modules:
  0.0 38.8 jit_solution(2563184469773714589)
XLA Ops:
  0.0 38.1 %shard_map.37 = f32[128,256]{1,0:T(8,128)S(1)} custom-call(f32[33,128,128]{2,1,0:T(8,128)} %bitcast.1, s32[1,33]{1,0:T(1,128)} %flags.1, f32[128,256]{1,0:T(8,128)} %orb.1), custom_call_target="tpu_custom_call" | custom-call | tf_op jit(solution)/shard_map/pallas_call | solution.py:431
  38.1 0.7 %copy.5 = f32[128,256]{1,0:T(8,128)} copy(f32[128,256]{1,0:T(8,128)S(1)} %shard_map.37) | data formatting | bytes 262144
